TPU v7x, 32 devices: a whole 2x2x4 slice. The times are simulated.
32 devices in a mesh: seq: 4 (over y, x), fsdp: 8 (over z, core).
Axes of the slice: x: 2, y: 2, z: 4, core: 2. Of those that a mesh axis runs over, the one named last changes fastest.
Arguments:
- block_input: bfloat16 [8, 2048, 1024], P('fsdp', 'seq'), may hold values from -6 to 6
- norm_gain_a: float32 [1024], P('fsdp'), may hold values from 0.1 to 1.9
- weight_qkv: float32 [1024, 3072], P('fsdp'), may hold values from -0.1875 to 0.1875
- weight_out: float32 [1024, 1024], P('fsdp'), may hold values from -3 to 3
- norm_gain_b: float32 [1024], P('fsdp'), may hold values from 0.1 to 1.9
- weight_gate_up: float32 [1024, 8192], P('fsdp'), may hold values from -0.1875 to 0.1875
- weight_down: float32 [1024, 4096], P('fsdp'), may hold values from -0.09375 to 0.09375
- cotangent: bfloat16 [8, 2048, 1024], P('fsdp', 'seq'), may hold values from -6 to 6
- permutation: int32 [8, 2048], P('fsdp'), may hold values from 0 to 2047, each once within a row
- lengths: int32 [8, 3], P('fsdp'), may hold values from 256 to 1024, as said below
- offsets: int32 [8, 3], P('fsdp'), may hold values from 0 to 1792, as said below
Outputs:
- block_output: bfloat16 [8, 2048, 1024], P('fsdp', 'seq')
- grad_input: bfloat16 [8, 2048, 1024], P('fsdp', 'seq')
- grad_gain_a: float32 [1024], P('fsdp')
- grad_qkv: float32 [1024, 3072], P('fsdp')
- grad_out: float32 [1024, 1024], P('fsdp')
- grad_gain_b: float32 [1024], P('fsdp')
- grad_gate_up: float32 [1024, 8192], P('fsdp')
- grad_down: float32 [1024, 4096], P('fsdp')
Inputs may be any that keep to these rules, and one draw needn't show every extreme that they name: A group's 3 lengths sum to 2048, and its longest is exactly 1024. offsets[g, k] is the sum of lengths[g, i] over i < k, so that a group's sequences tile its positions.
All inputs are finite; a program needn't handle non-finite values.
Results may differ from a plain program's by a relative error of at most 0.02.
Values may be sent and summed in bfloat16 or wider, within the bound.
A program may use at most 256 MiB of HBM per device.

v0:
```python
import jax
import jax.numpy as jnp
from jax import lax
from jax.sharding import PartitionSpec as P

HEADS = 16
HEAD_DIM = 64
epsilon = 1e-05


def rms_scale(values):
    return lax.rsqrt(jnp.mean(values * values, axis=-1, keepdims=True) + epsilon)


def norm_backward(values, inv_scale, grad_normed, gain):
    scaled = grad_normed * gain
    gain_grad = jnp.sum(grad_normed * values * inv_scale, axis=0)
    input_grad = inv_scale * scaled - values * inv_scale**3 * jnp.mean(
        values * scaled, axis=-1, keepdims=True
    )
    return (input_grad, gain_grad)


def block_mask(seg_query, pos_query, segment, position):
    return (seg_query[:, None] == segment[None, :]) & (position[None, :] <= pos_query[:, None])


def on_device(
    block_input,
    norm_gain_a,
    weight_qkv,
    weight_out,
    norm_gain_b,
    weight_gate_up,
    weight_down,
    cotangent,
    permutation,
    lengths,
    offsets,
):
    seq_count = lax.axis_size("seq")
    row_count = block_input.shape[1]
    model_width = block_input.shape[2]
    group_len = row_count * seq_count
    head_local = HEADS // seq_count
    score_scale = HEAD_DIM ** (-0.5)
    blk_rows = min(512, group_len)
    block_count = group_len // blk_rows
    inputs = block_input[0].astype(jnp.float32)
    gain_a, full_qkv, full_out = (
        lax.all_gather(norm_gain_a.astype(jnp.bfloat16), "fsdp", axis=0, tiled=True),
        lax.all_gather(weight_qkv.astype(jnp.bfloat16), "fsdp", axis=0, tiled=True),
        lax.all_gather(weight_out.astype(jnp.bfloat16), "fsdp", axis=0, tiled=True),
    )
    inv_first = rms_scale(inputs)
    normed_a = (inputs * inv_first * gain_a.astype(jnp.float32)).astype(jnp.bfloat16)
    qkv_rows = jnp.dot(normed_a, full_qkv, preferred_element_type=jnp.float32).astype(jnp.bfloat16)
    head_rows = lax.all_to_all(
        qkv_rows.reshape(row_count, 3, seq_count, -1),
        "seq",
        split_axis=2,
        concat_axis=0,
        tiled=True,
    )
    head_rows = head_rows.reshape(group_len, 3, head_local, HEAD_DIM)
    position = jnp.arange(group_len, dtype=jnp.int32)
    dealt_pos = permutation[0]
    inverse = jnp.zeros((group_len,), jnp.int32).at[dealt_pos].set(position)
    ordered = head_rows[inverse]
    seq_starts = offsets[0]
    seq_lengths = lengths[0]
    inside = (position[:, None] >= seq_starts[None, :]) & (
        position[:, None] < seq_starts[None, :] + seq_lengths[None, :]
    )
    segment = jnp.sum(
        inside.astype(jnp.int32) * jnp.arange(seq_lengths.shape[0], dtype=jnp.int32)[None, :],
        axis=1,
    )
    queries = ordered[:, 0]
    key_rows = ordered[:, 1]
    values = ordered[:, 2]

    def forward_block(block_item):
        query_blk, seg_blk, pos_blk = block_item
        scores = (
            jnp.einsum("qhd,khd->hqk", query_blk, key_rows, preferred_element_type=jnp.float32)
            * score_scale
        )
        allowed = block_mask(seg_blk, pos_blk, segment, position)
        scores = jnp.where(allowed[None], scores, -1e30)
        row_top = jnp.max(scores, axis=-1, keepdims=True)
        exponent = jnp.exp(scores - row_top)
        row_total = jnp.sum(exponent, axis=-1, keepdims=True)
        weights_low = (exponent / row_total).astype(jnp.bfloat16)
        attended = jnp.einsum(
            "hqk,khd->qhd", weights_low, values, preferred_element_type=jnp.float32
        )
        return (attended.astype(jnp.bfloat16), (row_top + jnp.log(row_total))[:, :, 0])

    query_blocks = queries.reshape(block_count, blk_rows, head_local, HEAD_DIM)
    seg_blocks = segment.reshape(block_count, blk_rows)
    pos_blocks = position.reshape(block_count, blk_rows)
    attended, log_total = lax.map(forward_block, (query_blocks, seg_blocks, pos_blocks))
    dealt_out = attended.reshape(group_len, -1)[dealt_pos]
    mixed = lax.all_to_all(
        dealt_out.reshape(group_len, 1, -1), "seq", split_axis=0, concat_axis=1, tiled=True
    ).reshape(row_count, model_width)
    hidden = inputs + jnp.dot(mixed, full_out, preferred_element_type=jnp.float32)
    gain_b, full_gate_up, full_down = (
        lax.all_gather(norm_gain_b.astype(jnp.bfloat16), "fsdp", axis=0, tiled=True),
        lax.all_gather(weight_gate_up.astype(jnp.bfloat16), "fsdp", axis=0, tiled=True),
        lax.all_gather(weight_down.astype(jnp.bfloat16), "fsdp", axis=0, tiled=True),
    )
    inv_second = rms_scale(hidden)
    normed_b = (hidden * inv_second * gain_b.astype(jnp.float32)).astype(jnp.bfloat16)
    gate_up = jnp.dot(normed_b, full_gate_up, preferred_element_type=jnp.float32)
    hidden_units = full_gate_up.shape[1] // 2
    gate_part = gate_up[:, :hidden_units]
    up_part = gate_up[:, hidden_units:]
    gate_sigmoid = jax.nn.sigmoid(gate_part)
    gate_silu = gate_part * gate_sigmoid
    activation = (gate_silu * up_part).astype(jnp.bfloat16)
    branch_out = jnp.einsum("rf,df->rd", activation, full_down, preferred_element_type=jnp.float32)
    result_rows = (hidden + branch_out).astype(jnp.bfloat16)
    gain_b, full_gate_up, full_down = (
        lax.all_gather(norm_gain_b.astype(jnp.bfloat16), "fsdp", axis=0, tiled=True),
        lax.all_gather(weight_gate_up.astype(jnp.bfloat16), "fsdp", axis=0, tiled=True),
        lax.all_gather(weight_down.astype(jnp.bfloat16), "fsdp", axis=0, tiled=True),
    )
    out_grad = cotangent[0].astype(jnp.float32)
    out_grad_low = out_grad.astype(jnp.bfloat16)
    grad_down_term = jnp.einsum(
        "rd,rf->df", out_grad_low, activation, preferred_element_type=jnp.float32
    )
    grad_activation = jnp.dot(out_grad_low, full_down, preferred_element_type=jnp.float32)
    grad_gate = grad_activation * up_part * gate_sigmoid * (1.0 + gate_part * (1.0 - gate_sigmoid))
    grad_up = grad_activation * gate_silu
    grad_gate_up = jnp.concatenate([grad_gate, grad_up], axis=1).astype(jnp.bfloat16)
    grad_gate_up_term = jnp.einsum(
        "rd,rf->df", normed_b, grad_gate_up, preferred_element_type=jnp.float32
    )
    grad_normed_b = jnp.einsum(
        "rf,df->rd", grad_gate_up, full_gate_up, preferred_element_type=jnp.float32
    )
    hidden_back, grad_gain_b_term = norm_backward(
        hidden, inv_second, grad_normed_b, gain_b.astype(jnp.float32)
    )
    grad_hidden = out_grad + hidden_back
    gain_a, full_qkv, full_out = (
        lax.all_gather(norm_gain_a.astype(jnp.bfloat16), "fsdp", axis=0, tiled=True),
        lax.all_gather(weight_qkv.astype(jnp.bfloat16), "fsdp", axis=0, tiled=True),
        lax.all_gather(weight_out.astype(jnp.bfloat16), "fsdp", axis=0, tiled=True),
    )
    grad_branch = grad_hidden.astype(jnp.bfloat16)
    grad_out_term = jnp.einsum("rd,re->de", mixed, grad_branch, preferred_element_type=jnp.float32)
    grad_mixed = jnp.einsum(
        "re,de->rd", grad_branch, full_out, preferred_element_type=jnp.float32
    ).astype(jnp.bfloat16)
    grad_heads = lax.all_to_all(
        grad_mixed.reshape(row_count, seq_count, -1), "seq", split_axis=1, concat_axis=0, tiled=True
    )
    grad_ordered = grad_heads.reshape(group_len, head_local, HEAD_DIM)[inverse]
    grad_blocks = grad_ordered.reshape(block_count, blk_rows, head_local, HEAD_DIM)

    def backward_block(carry, block_item):
        key_acc, value_acc = carry
        query_blk, grad_blk, log_blk, seg_blk, pos_blk = block_item
        scores = (
            jnp.einsum("qhd,khd->hqk", query_blk, key_rows, preferred_element_type=jnp.float32)
            * score_scale
        )
        allowed = block_mask(seg_blk, pos_blk, segment, position)
        scores = jnp.where(allowed[None], scores, -1e30)
        probability = jnp.exp(scores - log_blk[:, :, None])
        grad_prob = jnp.einsum("qhd,khd->hqk", grad_blk, values, preferred_element_type=jnp.float32)
        row_delta = jnp.sum(probability * grad_prob, axis=-1, keepdims=True)
        grad_score = (probability * (grad_prob - row_delta)).astype(jnp.bfloat16)
        grad_query = (
            jnp.einsum("hqk,khd->qhd", grad_score, key_rows, preferred_element_type=jnp.float32)
            * score_scale
        )
        key_acc = (
            key_acc
            + jnp.einsum("hqk,qhd->khd", grad_score, query_blk, preferred_element_type=jnp.float32)
            * score_scale
        )
        value_acc = value_acc + jnp.einsum(
            "hqk,qhd->khd",
            probability.astype(jnp.bfloat16),
            grad_blk,
            preferred_element_type=jnp.float32,
        )
        return ((key_acc, value_acc), grad_query.astype(jnp.bfloat16))

    zero_acc = jnp.zeros((group_len, head_local, HEAD_DIM), jnp.float32)
    accumulated, query_grad = lax.scan(
        backward_block,
        (zero_acc, zero_acc),
        (query_blocks, grad_blocks, log_total, seg_blocks, pos_blocks),
    )
    qkv_grad = jnp.stack(
        [
            query_grad.reshape(group_len, -1),
            accumulated[0].reshape(group_len, -1).astype(jnp.bfloat16),
            accumulated[1].reshape(group_len, -1).astype(jnp.bfloat16),
        ],
        axis=1,
    )
    dealt_grad = qkv_grad[dealt_pos]
    rows_grad = lax.all_to_all(
        dealt_grad.reshape(group_len, 3, 1, -1), "seq", split_axis=0, concat_axis=2, tiled=True
    ).reshape(row_count, -1)
    grad_qkv_term = jnp.einsum("rd,re->de", normed_a, rows_grad, preferred_element_type=jnp.float32)
    grad_normed_a = jnp.einsum("re,de->rd", rows_grad, full_qkv, preferred_element_type=jnp.float32)
    input_back, grad_gain_a_term = norm_backward(
        inputs, inv_first, grad_normed_a, gain_a.astype(jnp.float32)
    )
    input_grad = (grad_hidden + input_back).astype(jnp.bfloat16)
    attn_shards = (
        lax.psum_scatter(
            grad_gain_a_term.astype(jnp.bfloat16), "fsdp", scatter_dimension=0, tiled=True
        ).astype(jnp.float32),
        lax.psum_scatter(
            grad_qkv_term.astype(jnp.bfloat16), "fsdp", scatter_dimension=0, tiled=True
        ).astype(jnp.float32),
        lax.psum_scatter(
            grad_out_term.astype(jnp.bfloat16), "fsdp", scatter_dimension=0, tiled=True
        ).astype(jnp.float32),
    )
    mlp_shards = (
        lax.psum_scatter(
            grad_gain_b_term.astype(jnp.bfloat16), "fsdp", scatter_dimension=0, tiled=True
        ).astype(jnp.float32),
        lax.psum_scatter(
            grad_gate_up_term.astype(jnp.bfloat16), "fsdp", scatter_dimension=0, tiled=True
        ).astype(jnp.float32),
        lax.psum_scatter(
            grad_down_term.astype(jnp.bfloat16), "fsdp", scatter_dimension=0, tiled=True
        ).astype(jnp.float32),
    )
    totals = (
        lax.psum(attn_shards[0].astype(jnp.bfloat16), "seq").astype(jnp.float32),
        lax.psum(attn_shards[1].astype(jnp.bfloat16), "seq").astype(jnp.float32),
        lax.psum(attn_shards[2].astype(jnp.bfloat16), "seq").astype(jnp.float32),
        lax.psum(mlp_shards[0].astype(jnp.bfloat16), "seq").astype(jnp.float32),
        lax.psum(mlp_shards[1].astype(jnp.bfloat16), "seq").astype(jnp.float32),
        lax.psum(mlp_shards[2].astype(jnp.bfloat16), "seq").astype(jnp.float32),
    )
    return (
        result_rows[None],
        input_grad[None],
        totals[0],
        totals[1],
        totals[2],
        totals[3],
        totals[4],
        totals[5],
    )


def solution(mesh):
    placed = (
        P("fsdp", "seq", None),
        P("fsdp"),
        P("fsdp", None),
        P("fsdp", None),
        P("fsdp"),
        P("fsdp", None),
        P("fsdp", None),
        P("fsdp", "seq", None),
        P("fsdp", None),
        P("fsdp", None),
        P("fsdp", None),
    )
    return jax.shard_map(
        on_device,
        mesh=mesh,
        in_specs=placed,
        out_specs=(
            P("fsdp", "seq", None),
            P("fsdp", "seq", None),
            P("fsdp"),
            P("fsdp", None),
            P("fsdp", None),
            P("fsdp"),
            P("fsdp", None),
            P("fsdp", None),
        ),
        check_vma=False,
    )
```

profile of v0, /device:TPU:0, one launch (start us, length us, event | category | flops | bytes accessed | tf_op | source)
XLA Modules:
  0.0 1127.1 jit_solution(276207675843231154)
XLA Ops:
  15.4 13.5 %all-gather = bf16[8,1,128]{2,1,0:T(2,128)(2,1)S(1)} all-gather(bf16[1,1,128]{2,1,0:T(2,128)(2,1)S(1)} %convert_bitcast_fusion.3), channel_id=1, replica_groups=mesh['seq'=4,'fsdp'=8] {'fsdp'}, dimensions={0}, use_global_device_ids=true | all-gather | bytes 2304 | tf_op jit(solution)/shard_map/all_gather | solution.py:51
  29.8 47.9 %all-gather.7.cloned.1.call-done = bf16[1024,3072]{1,0:T(8,128)(2,1)} async-done(((bf16[128,3072]{1,0:T(8,128)(2,1)}), bf16[1024,3072]{1,0:T(8,128)(2,1)}) %all-gather.7.cloned.1.call-update) | async-done | bytes 6291472 | tf_op jit(solution)/shard_map/all_gather | solution.py:52
  112.3 23.5 %all-to-all-done = bf16[512,3,4,256]{0,3,1,2:T(8,128)(2,1)S(1)} async-done(((bf16[512,3,4,256]{0,3,1,2:T(8,128)(2,1)}), bf16[512,3,4,256]{0,3,1,2:T(8,128)(2,1)S(1)}, u32[]{:S(2)}, u32[]{:S(2)}) %all-to-all-start) | async-done | bytes 3145760 | tf_op jit(solution)/shard_map/all_to_all | solution.py:58
  140.4 13.1 %reshape.380 = bf16[2048,3,4,64]{3,2,1,0:T(4,128)(2,1)} reshape(bf16[4,512,3,1,256]{4,2,1,0,3:T(4,128)(2,1)} %copy.141) | data formatting | bytes 6291456 | tf_op jit(solution)/shard_map/reshape | solution.py:65
  153.6 23.0 %gather_fusion = bf16[2048,3,4,64]{3,2,1,0:T(4,128)(2,1)} fusion(bf16[2048,3,4,64]{3,2,1,0:T(4,128)(2,1)} %reshape.380, s32[2048]{0:T(1024)S(1)} %fusion.84), kind=kCustom, calls=%fused_computation | custom fusion | bytes 6299648 | tf_op jit(solution)/shard_map/gather | solution.py:69
  191.8 64.2 %while.28 = (s32[]{:T(128)}, bf16[4,512,4,64]{1,3,2,0:T(8,128)(2,1)}, f32[4,4,512]{2,1,0:T(4,128)}, s32[4,512]{1,0:T(4,128)}, s32[2048]{0:T(1024)S(1)}, /*index=...) while((s32[]{:T(128)}, ...), condition=%wide.region_6.7_spmd.clone, body=%wide.region_3.6_spmd.clone.sunk | while | flops 1127348224 | bytes 57233532 | solution.py:103
  282.9 9.8 all-gather.1
  310.1 18.8 %fusion.89 = f32[512,8192]{1,0:T(8,128)} fusion(bf16[1024,8192]{1,0:T(8,128)(2,1)} %all-gather.11.cloned.1.call-done, f32[512,1024]{1,0:T(8,128)} %get-tuple-element.422, f32[1024]{0:T(1024)S(1)} %bitcast.234, f32[512]{0:T(512)S(1)} %get-tuple-element.420), kind=kOutput, calls=%fused_computation.139 | convolution fusion | flops 8591507456 | bytes 35657728 | tf_op jit(solution)/shard_map/dot_general | solution.py:116
  328.9 13.4 %all-gather.13.cloned.1.call-done = bf16[1024,4096]{1,0:T(8,128)(2,1)} async-done(((bf16[128,4096]{1,0:T(8,128)(2,1)}), bf16[1024,4096]{1,0:T(8,128)(2,1)}) %all-gather.13.cloned.1.call-update) | async-done | bytes 8388624 | tf_op jit(solution)/shard_map/all_gather | solution.py:112
  342.3 15.1 %multiply_convert_fusion.2 = (bf16[512,4096]{1,0:T(8,128)(2,1)}, bf16[512,4096]{1,0:T(8,128)(2,1)}, bf16[512,4096]{1,0:T(8,128)(2,1)S(1)}) fusion(f32[512,8192]{1,0:T(8,128)} %fusion.89, bf16[1024,4096]{1,0:T(8,128)(2,1)} %all-gather.13.cloned.1.call-done, bf16[1,512,1024]{2,1,0:T(8,128)(2,1)S(1)} %copy-done.22), kind=kOutput, calls=%fused_computation.67 | convolution fusion | flops 4326424576 | bytes 38797312 | tf_op jit(solution)/shard_map/dot_general | solution.py:135
  366.2 11.7 %copy.151 = bf16[1024,4096]{1,0:T(8,128)(2,1)} copy(bf16[1024,4096]{0,1:T(8,128)(2,1)} %convert_bitcast_fusion) | data formatting | bytes 16777216
  377.9 18.0 %multiply_reduce_fusion.1 = (bf16[1024]{0:T(1024)(128)(2,1)}, f32[512]{0:T(512)S(1)}, f32[512,1024]{1,0:T(8,128)}) fusion(f32[512,1024]{1,0:T(8,128)} %get-tuple-element.422, f32[512]{0:T(512)S(1)} %get-tuple-element.420, f32[1024]{0:T(1024)S(1)} %bitcast.235, bf16[1024,8192]{1,0:T(8,128)(2,1)} %all-gather.11.cloned.1.call-done, ...), kind=kOutput, calls=%fused_computation.97 | convolution fusion | flops 8609855488 | bytes 29370368 | tf_op jit(solution)/shard_map/rf,df->rd/dot_general | solution.py:142
  411.2 9.6 all-to-all-done.2
  425.0 16.1 %gather_fusion.2 = bf16[2048,4,64]{2,1,0:T(4,128)(2,1)} fusion(bf16[2048,4,64]{2,1,0:T(4,128)(2,1)} %reshape.382, s32[2048]{0:T(1024)S(1)} %copy-done.27), kind=kCustom, calls=%fused_computation.2 | custom fusion | bytes 2105344 | tf_op jit(solution)/shard_map/gather | solution.py:162
  446.2 209.1 %while.29 = (s32[]{:T(128)}, f32[2048,4,64]{0,2,1:T(8,128)}, f32[2048,4,64]{0,2,1:T(8,128)}, bf16[4,512,4,64]{1,3,2,0:T(8,128)(2,1)}, bf16[4,512,4,64]{1,3,2,0:T...) while((s32[]{:T(128)}, f32[2048,4,64]{0,2,1:T(8,128)}, ...), condition=%wide.region_11.12_spmd.clone, body=%wide.region_9.11_spmd.clone.sunk | while | flops 2753296384 | bytes 268841472 | solution.py:196
  454.4 12.3 %multiply_reduce_fusion.5 = (f32[4,512]{1,0:T(4,128)}, f32[4,512,2048]{2,1,0:T(8,128)}) fusion(f32[4,512,2048]{2,1,0:T(8,128)S(1)} %fusion.146, f32[4,512]{1,0:T(4,128)S(1)} %dynamic-slice_bitcast_fusion.2, pred[512,2048]{1,0:T(8,128)(4,1)S(1)} %fusion.147, bf16[2048,4,64]{0,2,1:T(8,128)(2,1)} %get-tuple-element.638, ...), kind=kOutput, calls=%fused_computation.28.clone.1 | convolution fusion | flops 557840384 | bytes 35930116 | tf_op jit(solution)/shard_map/while/body/eval_jaxpr/qhd,khd->hqk/dot_general | solution.py:175
  466.7 11.0 multiply_convert_fusion.8
  506.3 12.3 %multiply_reduce_fusion.5 = (f32[4,512]{1,0:T(4,128)}, f32[4,512,2048]{2,1,0:T(8,128)}) fusion(f32[4,512,2048]{2,1,0:T(8,128)S(1)} %fusion.146, f32[4,512]{1,0:T(4,128)S(1)} %dynamic-slice_bitcast_fusion.2, pred[512,2048]{1,0:T(8,128)(4,1)S(1)} %fusion.147, bf16[2048,4,64]{0,2,1:T(8,128)(2,1)} %get-tuple-element.638, ...), kind=kOutput, calls=%fused_computation.28.clone.1 | convolution fusion | flops 557840384 | bytes 35930116 | tf_op jit(solution)/shard_map/while/body/eval_jaxpr/qhd,khd->hqk/dot_general | solution.py:175
  518.6 10.9 multiply_convert_fusion.8
  558.5 12.3 %multiply_reduce_fusion.5 = (f32[4,512]{1,0:T(4,128)}, f32[4,512,2048]{2,1,0:T(8,128)}) fusion(f32[4,512,2048]{2,1,0:T(8,128)S(1)} %fusion.146, f32[4,512]{1,0:T(4,128)S(1)} %dynamic-slice_bitcast_fusion.2, pred[512,2048]{1,0:T(8,128)(4,1)S(1)} %fusion.147, bf16[2048,4,64]{0,2,1:T(8,128)(2,1)} %get-tuple-element.638, ...), kind=kOutput, calls=%fused_computation.28.clone.1 | convolution fusion | flops 557840384 | bytes 35930116 | tf_op jit(solution)/shard_map/while/body/eval_jaxpr/qhd,khd->hqk/dot_general | solution.py:175
  570.8 10.9 multiply_convert_fusion.8
  610.7 12.3 %multiply_reduce_fusion.5 = (f32[4,512]{1,0:T(4,128)}, f32[4,512,2048]{2,1,0:T(8,128)}) fusion(f32[4,512,2048]{2,1,0:T(8,128)S(1)} %fusion.146, f32[4,512]{1,0:T(4,128)S(1)} %dynamic-slice_bitcast_fusion.2, pred[512,2048]{1,0:T(8,128)(4,1)S(1)} %fusion.147, bf16[2048,4,64]{0,2,1:T(8,128)(2,1)} %get-tuple-element.638, ...), kind=kOutput, calls=%fused_computation.28.clone.1 | convolution fusion | flops 557840384 | bytes 35930116 | tf_op jit(solution)/shard_map/while/body/eval_jaxpr/qhd,khd->hqk/dot_general | solution.py:175
  623.0 10.9 multiply_convert_fusion.8
  686.7 18.7 %gather_fusion.3 = bf16[2048,3,256]{2,1,0:T(4,128)(2,1)} fusion(bf16[2048,3,256]{2,1,0:T(4,128)(2,1)} %pad_maximum_fusion.3, s32[2048]{0:T(1024)S(1)} %copy-done.25), kind=kCustom, calls=%fused_computation.3 | custom fusion | bytes 6299648 | tf_op jit(solution)/shard_map/gather | solution.py:209
  705.4 51.5 %all_to_all.60 = bf16[2048,3,1,256]{3,1,2,0:T(4,128)(2,1)S(1)} all-to-all(bf16[2048,3,1,256]{3,1,2,0:T(4,128)(2,1)} %bitcast.213), channel_id=1, replica_groups=mesh['seq'=4,'fsdp'=8] {'seq'}, dimensions={0} | all-to-all | bytes 6291456 | tf_op jit(solution)/shard_map/all_to_all | solution.py:210
  770.4 16.6 %convolution_convert_fusion = bf16[1024,8192]{1,0:T(8,128)(2,1)} fusion(bf16[512,4096]{1,0:T(8,128)(2,1)} %get-tuple-element.412, bf16[512,4096]{1,0:T(8,128)(2,1)} %get-tuple-element.411, f32[512,1024]{1,0:T(8,128)S(1)} %copy-done.12, f32[1024]{0:T(1024)S(1)} %bitcast.237, f32[512]{0:T(512)S(1)} %copy-done.36), kind=kOutput, calls=%fused_computation.63 | convolution fusion | flops 8616673280 | bytes 27269120 | tf_op jit(solution)/shard_map/rd,rf->df/dot_general | solution.py:139
  789.6 45.9 %reduce-scatter.7.cloned.1.call-done = bf16[128,3072]{1,0:T(8,128)(2,1)} async-done(((bf16[1024,3072]{1,0:T(8,128)(2,1)}), bf16[128,3072]{1,0:T(8,128)(2,1)}) %reduce-scatter.7.cloned.1.call-update) | async-done | bytes 786448 | tf_op jit(solution)/shard_map/reduce_scatter | solution.py:223
  835.4 169.0 %reduce-scatter.11.cloned.1.call-done = bf16[128,8192]{1,0:T(8,128)(2,1)} async-done(((bf16[1024,8192]{1,0:T(8,128)(2,1)}), bf16[128,8192]{1,0:T(8,128)(2,1)}) %reduce-scatter.11.cloned.1.call-update) | async-done | bytes 2097168 | tf_op jit(solution)/shard_map/reduce_scatter | solution.py:234
  1005.7 10.3 fusion.69
  1024.0 13.6 %all-reduce.2 = (bf16[1024]{0:T(1024)(128)(2,1)S(1)}, bf16[1024]{0:T(1024)(128)(2,1)S(1)}) all-reduce(bf16[1024]{0:T(1024)(128)(2,1)S(1)} %get-tuple-element.351, bf16[1024]{0:T(1024)(128)(2,1)S(1)} %copy-done.38), channel_id=2, replica_groups=mesh['seq'=4,'fsdp'=8] {'fsdp'}, use_global_device_ids=true, to_apply=%region_14.15.clone | all-reduce | flops 2048 | bytes 8192
  1037.8 10.2 all-reduce.3
  1052.1 59.8 %all-reduce.7.cloned.1.call-done = (bf16[128,4096]{0,1:T(8,128)(2,1)}, bf16[128,3072]{1,0:T(8,128)(2,1)}, bf16[128,1024]{1,0:T(8,128)(2,1)}, bf16[128,8192]{1,0:T(8,128)(2,1)}) async-done(((bf16[128,4096]{0,1:T(8,128)(2,1)}, bf16[128,3072]{1,0:T(8,128)(2,1)}, bf16[128,1024]{1,0:T(8,128)(2,1)}, bf16[128,8192]{1,0:T(8,128)(2,1)}), (bf16[128,4096]{0,1:T(8,128)(2,1)}, bf16[128,3072]{1,0:T(8,128)(2,1)}, ...) | async-done | bytes 4194320 | tf_op jit(solution)/shard_map/psum | solution.py:247
  (317 shorter events, 388.9 us)
Async XLA Ops:
  7.2 70.6 %all-gather.7.cloned.1.call-start = ((), (), s32[]{:S(2)}) async-start(), calls=%async_computation.8 | async-start | bytes 7077888 | tf_op jit(solution)/shard_map/all_gather | solution.py:52
  9.6 295.9 %all-gather.9.cloned.1.call-start = ((), (), s32[]{:S(2)}) async-start(), calls=%async_computation.9 | async-start | bytes 2359296 | tf_op jit(solution)/shard_map/all_gather | solution.py:53
  11.5 17.4 %copy-start.7 = (bf16[1,512,1024]{2,1,0:T(8,128)(2,1)S(1)}, bf16[1,512,1024]{2,1,0:T(8,128)(2,1)}, u32[]{:S(2)}) copy-start(bf16[1,512,1024]{2,1,0:T(8,128)(2,1)} %param.15) | copy-start | bytes 3145732
  11.5 298.6 %all-gather.11.cloned.1.call-start = ((), (), s32[]{:S(2)}) async-start(), calls=%async_computation.10 | async-start | bytes 18874368 | tf_op jit(solution)/shard_map/all_gather | solution.py:111
  28.9 48.8 %copy-start.30 = (f32[8,1,128]{2,1,0:T(1,128)}, f32[8,1,128]{2,1,0:T(1,128)S(1)}, u32[]{:S(2)}) copy-start(f32[8,1,128]{2,1,0:T(1,128)S(1)} %convert_element_type.214) | copy-start | bytes 12292
  29.8 47.9 %copy-start.33 = (f32[512]{0:T(512)}, f32[512]{0:T(512)S(1)}, u32[]{:S(2)}) copy-start(f32[512]{0:T(512)S(1)} %get-tuple-element.418) | copy-start | bytes 6148
  95.2 40.6 %all-to-all-start = ((bf16[512,3,4,256]{0,3,1,2:T(8,128)(2,1)}), bf16[512,3,4,256]{0,3,1,2:T(8,128)(2,1)S(1)}, u32[]{:S(2)}, u32[]{:S(2)}) async-start(bf16[512,3,4,256]{0,3,1,2:T(8,128)(2,1)} %copy.114), calls=%async_computation | async-start | bytes 6291456 | tf_op jit(solution)/shard_map/all_to_all | solution.py:58
  99.1 243.2 %all-gather.13.cloned.1.call-start = ((), (), s32[]{:S(2)}) async-start(), calls=%async_computation.11 | async-start | bytes 9437184 | tf_op jit(solution)/shard_map/all_gather | solution.py:112
  112.3 41.2 %copy-start.26 = (s32[2048]{0:T(1024)}, s32[2048]{0:T(1024)S(1)}, u32[]{:S(2)}) copy-start(s32[2048]{0:T(1024)S(1)} %fusion.84) | copy-start | bytes 24580
  278.5 17.8 %all-to-all-start.1 = ((bf16[4,2,65536]{2,1,0:T(2,128)(2,1)}), bf16[4,2,65536]{2,1,0:T(2,128)(2,1)}, u32[]{:S(2)}, u32[]{:S(2)}) async-start(bf16[4,2,65536]{2,1,0:T(2,128)(2,1)} %reshape.393), calls=%async_computation.1 | async-start | bytes 2097152 | tf_op jit(solution)/shard_map/all_to_all | solution.py:105
  282.8 504.3 %reduce-scatter.13.cloned.1.call-start = ((), (), s32[]{:S(2)}) async-start(), calls=%async_computation.15 | async-start | bytes 9437184
  292.7 103.2 %copy-start.28 = (f32[8,1,128]{2,1,0:T(1,128)}, f32[8,1,128]{2,1,0:T(1,128)S(1)}, u32[]{:S(2)}) copy-start(f32[8,1,128]{2,1,0:T(1,128)S(1)} %convert_element_type.215) | copy-start | bytes 12292
  292.7 12.8 %copy-start.8 = (bf16[1,512,1024]{2,1,0:T(8,128)(2,1)S(1)}, bf16[1,512,1024]{2,1,0:T(8,128)(2,1)}, u32[]{:S(2)}) copy-start(bf16[1,512,1024]{2,1,0:T(8,128)(2,1)} %param.15) | copy-start | bytes 3145732
  310.0 85.9 %copy-start.35 = (f32[512]{0:T(512)}, f32[512]{0:T(512)S(1)}, u32[]{:S(2)}) copy-start(f32[512]{0:T(512)S(1)} %get-tuple-element.420) | copy-start | bytes 6148
  310.1 32.2 %copy-start.22 = (bf16[1,512,1024]{2,1,0:T(8,128)(2,1)S(1)}, bf16[1,512,1024]{2,1,0:T(8,128)(2,1)}, u32[]{:S(2)}) copy-start(bf16[1,512,1024]{2,1,0:T(8,128)(2,1)} %param.22) | copy-start | bytes 3145732
  402.8 17.9 %all-to-all-start.2 = ((bf16[512,4,256]{0,2,1:T(8,128)(2,1)}), bf16[512,4,256]{0,2,1:T(8,128)(2,1)S(1)}, u32[]{:S(2)}, u32[]{:S(2)}) async-start(bf16[512,4,256]{0,2,1:T(8,128)(2,1)} %bitcast.222), calls=%async_computation.2 | async-start | bytes 2097152 | tf_op jit(solution)/shard_map/all_to_all | solution.py:159
  406.5 383.0 %reduce-scatter.9.cloned.1.call-start = ((), (), s32[]{:S(2)}) async-start(), calls=%async_computation.13 | async-start | bytes 2359296 | tf_op jit(solution)/shard_map/reduce_scatter | solution.py:226
  411.1 13.9 %copy-start.27 = (s32[2048]{0:T(1024)S(1)}, s32[2048]{0:T(1024)}, u32[]{:S(2)}) copy-start(s32[2048]{0:T(1024)} %copy-done.26) | copy-start | bytes 24580
  411.1 424.3 %reduce-scatter.7.cloned.1.call-start = ((), (), s32[]{:S(2)}) async-start(), calls=%async_computation.12 | async-start | bytes 7077888 | tf_op jit(solution)/shard_map/reduce_scatter | solution.py:223
  450.9 15.8 %copy-start = (f32[4,512,2048]{2,1,0:T(8,128)}, f32[4,512,2048]{2,1,0:T(8,128)S(1)}, u32[]{:S(2)}) copy-start(f32[4,512,2048]{2,1,0:T(8,128)S(1)} %fusion.146) | copy-start | bytes 50331652 | tf_op jit(solution)/shard_map/while
  477.7 15.3 %slice-start = ((s8[8388608]{0:T(1024)(128)(4,1)}), s8[4194304]{0:T(1024)(128)(4,1)S(1)}, s32[]{:S(2)}) async-start(s8[8388608]{0:T(1024)(128)(4,1)} %bitcast.211), calls=%async_computation.17 | async-start | bytes 8388608 | tf_op jit(solution)/shard_map/while
  502.8 15.8 %copy-start = (f32[4,512,2048]{2,1,0:T(8,128)}, f32[4,512,2048]{2,1,0:T(8,128)S(1)}, u32[]{:S(2)}) copy-start(f32[4,512,2048]{2,1,0:T(8,128)S(1)} %fusion.146) | copy-start | bytes 50331652 | tf_op jit(solution)/shard_map/while
  529.5 15.7 %slice-start = ((s8[8388608]{0:T(1024)(128)(4,1)}), s8[4194304]{0:T(1024)(128)(4,1)S(1)}, s32[]{:S(2)}) async-start(s8[8388608]{0:T(1024)(128)(4,1)} %bitcast.211), calls=%async_computation.17 | async-start | bytes 8388608 | tf_op jit(solution)/shard_map/while
  555.0 15.8 %copy-start = (f32[4,512,2048]{2,1,0:T(8,128)}, f32[4,512,2048]{2,1,0:T(8,128)S(1)}, u32[]{:S(2)}) copy-start(f32[4,512,2048]{2,1,0:T(8,128)S(1)} %fusion.146) | copy-start | bytes 50331652 | tf_op jit(solution)/shard_map/while
  581.8 15.7 %slice-start = ((s8[8388608]{0:T(1024)(128)(4,1)}), s8[4194304]{0:T(1024)(128)(4,1)S(1)}, s32[]{:S(2)}) async-start(s8[8388608]{0:T(1024)(128)(4,1)} %bitcast.211), calls=%async_computation.17 | async-start | bytes 8388608 | tf_op jit(solution)/shard_map/while
  607.2 15.8 %copy-start = (f32[4,512,2048]{2,1,0:T(8,128)}, f32[4,512,2048]{2,1,0:T(8,128)S(1)}, u32[]{:S(2)}) copy-start(f32[4,512,2048]{2,1,0:T(8,128)S(1)} %fusion.146) | copy-start | bytes 50331652 | tf_op jit(solution)/shard_map/while
  634.0 15.7 %slice-start = ((s8[8388608]{0:T(1024)(128)(4,1)}), s8[4194304]{0:T(1024)(128)(4,1)S(1)}, s32[]{:S(2)}) async-start(s8[8388608]{0:T(1024)(128)(4,1)} %bitcast.211), calls=%async_computation.17 | async-start | bytes 8388608 | tf_op jit(solution)/shard_map/while
  768.8 235.6 %reduce-scatter.11.cloned.1.call-start = ((), (), s32[]{:S(2)}) async-start(), calls=%async_computation.14 | async-start | bytes 18874368 | tf_op jit(solution)/shard_map/reduce_scatter | solution.py:234
  787.0 217.4 %copy-start.43 = (u32[32]{0:T(128)S(1)}, u32[32]{0:T(128)}, u32[]{:S(2)}) copy-start(u32[32]{0:T(128)} %constant.73) | copy-start | bytes 388
  787.0 324.9 %all-reduce.7.cloned.1.call-start = ((), (), s32[]{:S(2)}) async-start(), calls=%async_computation.16 | async-start | bytes 8388608 | tf_op jit(solution)/shard_map/psum | solution.py:247
  1016.0 33.0 %copy-start.11 = (f32[512,1024]{1,0:T(8,128)S(1)}, f32[512,1024]{1,0:T(8,128)}, u32[]{:S(2)}) copy-start(f32[512,1024]{1,0:T(8,128)} %copy-done.10) | copy-start | bytes 6291460
  1016.0 33.0 %copy-start.32 = (f32[512]{0:T(512)S(1)}, f32[512]{0:T(512)}, u32[]{:S(2)}) copy-start(f32[512]{0:T(512)} %get-tuple-element.417) | copy-start | bytes 6148
  (60 other events, 317.0 us)
Sparse Core Ops, SparseCore 0:
  10.2 67.4 all-gather.6
  79.9 27.7 all-gather.8
  109.3 150.5 all-gather.10
  261.9 80.2 all-gather.12
  378.0 88.1 reduce-scatter.12
  468.4 34.2 reduce-scatter.8
  768.9 66.4 reduce-scatter.6
  837.8 166.5 reduce-scatter.10
  1008.7 103.2 all-reduce.6
where the time goes:
time: 1140 us; the launch traced here: 1130 us
  waiting for transfers between devices  373 us (33%)
  matrix products  303 us (27%)
  local copies, waits for them, and re-layouts  207 us (18%)
  other arithmetic  117 us (10%)
  blocking collectives  98.6 us (9%)
  between operations  15.1 us (1%)
  starting transfers between devices  12.2 us (1%)
    reduce_scatter x1, waiting for transfers between devices, on_device(): lax.psum_scatter(grad_gate_up_term.astype(jnp.bfloat16), 'fsdp', scatter_...  169 us
    psum x1, waiting for transfers between devices, on_device(): lax.psum(mlp_shards[2].astype(jnp.bfloat16), 'seq').astype(jnp.float32)  59.8 us
    all_to_all x1, blocking collectives, on_device(): lax.all_to_all(dealt_grad.reshape(group_len, 3, 1, -1), 'seq', split_axis...  51.5 us
    dot_general x4, matrix products, backward_block(): jnp.einsum('qhd,khd->hqk', grad_blk, values, preferred_element_type=jnp.f...  49.3 us
    all_gather x1, waiting for transfers between devices, on_device(): lax.all_gather(weight_qkv.astype(jnp.bfloat16), 'fsdp', axis=0, tiled=True)  47.9 us
    reduce_scatter x1, waiting for transfers between devices, on_device(): lax.psum_scatter(grad_qkv_term.astype(jnp.bfloat16), 'fsdp', scatter_dime...  45.9 us
    unnamed x85, local copies, waits for them, and re-layouts  44.8 us
    convert_element_type x4, other arithmetic, backward_block(): grad_score = (probability * (grad_prob - row_delta)).astype(jnp.bfloat16)  43.7 us
  transfers between devices with their start and end apart: 12, of which 8 were waited for; matrix products, arithmetic and copies ran while one was open for 51% of the time, Pallas kernels for 0%

commit v1 on v0

--- a/solution.py
+++ b/solution.py
@@ -6,6 +6,17 @@
 HEADS = 16
 HEAD_DIM = 64
 epsilon = 1e-05
+
+
+def in_blocks(x, dim, peers):
+    before, after = (x.shape[:dim], x.shape[dim + 1 :])
+    return jnp.moveaxis(x.reshape(*before, peers, -1, *after), dim, 0)
+
+
+def laid_out(blocks, dim):
+    blocks = jnp.moveaxis(blocks, 0, dim)
+    lengths = blocks.shape
+    return blocks.reshape(*lengths[:dim], lengths[dim] * lengths[dim + 1], *lengths[dim + 2 :])
 
 
 def rms_scale(values):
@@ -55,13 +66,15 @@
     inv_first = rms_scale(inputs)
     normed_a = (inputs * inv_first * gain_a.astype(jnp.float32)).astype(jnp.bfloat16)
     qkv_rows = jnp.dot(normed_a, full_qkv, preferred_element_type=jnp.float32).astype(jnp.bfloat16)
-    head_rows = lax.all_to_all(
-        qkv_rows.reshape(row_count, 3, seq_count, -1),
-        "seq",
-        split_axis=2,
-        concat_axis=0,
-        tiled=True,
-    )
+    x = qkv_rows.reshape(row_count, 3, seq_count, -1)
+    count, mine = (lax.axis_size("seq"), lax.axis_index("seq"))
+    pieces = in_blocks(x, 2, count)
+    gathered = [pieces[mine]]
+    for hop in range(1, count):
+        sent = pieces[mine ^ hop]
+        gathered.append(lax.ppermute(sent, "seq", [(i, i ^ hop) for i in range(count)]))
+    pieces = jnp.stack(gathered)[mine ^ jnp.arange(count)]
+    head_rows = laid_out(pieces, 0)
     head_rows = head_rows.reshape(group_len, 3, head_local, HEAD_DIM)
     position = jnp.arange(group_len, dtype=jnp.int32)
     dealt_pos = permutation[0]

time: 1140 us -> 1140 us (level)
    another operation x2 -> x6, local copies, waits for them, and re-layouts: 2.15 us -> 32.8 us  [the longest x2 17.8 us: on_device(): head_rows = head_rows.reshape(group_len, 3, head_local, HEAD_DIM)]
    reshape x4 -> x0, local copies, waits for them, and re-layouts: 27.5 us -> none  [the longest x2 17.8 us: on_device(): head_rows = head_rows.reshape(group_len, 3, head_local, HEAD_DIM)]
    all_to_all x1 -> x0, waiting for transfers between devices: 23.5 us -> none  [on_device(): lax.all_to_all(qkv_rows.reshape(row_count, 3, seq_count, -1), 'seq', spli...]
    ppermute x0 -> x3, waiting for transfers between devices: none -> 22 us  [on_device(): lax.ppermute(sent, 'seq', [(i, i ^ hop) for i in range(count)])]
    unnamed x85 -> x93, local copies, waits for them, and re-layouts: 44.8 us -> 48.1 us
  transfers between devices with their start and end apart: 12 -> 14, of which waited for: 8 -> 10; matrix products, arithmetic and copies ran while one was open for 51% -> 52% of each run, Pallas kernels for 0% -> 0%
where the time goes in v1:
time: 1140 us; the launch traced here: 1130 us
  waiting for transfers between devices  363 us (32%)
  matrix products  304 us (27%)
  local copies, waits for them, and re-layouts  216 us (19%)
  other arithmetic  118 us (10%)
  blocking collectives  98 us (9%)
  between operations  15.4 us (1%)
  starting transfers between devices  11.7 us (1%)
    reduce_scatter x1, waiting for transfers between devices, on_device(): lax.psum_scatter(grad_gate_up_term.astype(jnp.bfloat16), 'fsdp', scatter_...  169 us
    psum x1, waiting for transfers between devices, on_device(): lax.psum(mlp_shards[2].astype(jnp.bfloat16), 'seq').astype(jnp.float32)  59.8 us
    all_to_all x1, blocking collectives, on_device(): lax.all_to_all(dealt_grad.reshape(group_len, 3, 1, -1), 'seq', split_axis...  51.6 us
    dot_general x4, matrix products, backward_block(): jnp.einsum('qhd,khd->hqk', grad_blk, values, preferred_element_type=jnp.f...  49.2 us
    unnamed x93, local copies, waits for them, and re-layouts  48.1 us
    all_gather x1, waiting for transfers between devices, on_device(): lax.all_gather(weight_qkv.astype(jnp.bfloat16), 'fsdp', axis=0, tiled=True)  46.5 us
    reduce_scatter x1, waiting for transfers between devices, on_device(): lax.psum_scatter(grad_qkv_term.astype(jnp.bfloat16), 'fsdp', scatter_dime...  45.8 us
    convert_element_type x4, other arithmetic, backward_block(): grad_score = (probability * (grad_prob - row_delta)).astype(jnp.bfloat16)  43.6 us
  transfers between devices with their start and end apart: 14, of which 10 were waited for; matrix products, arithmetic and copies ran while one was open for 52% of the time, Pallas kernels for 0%

profile of v1, /device:TPU:0, one launch (start us, length us, event | category | flops | bytes accessed | tf_op | source)
XLA Modules:
  0.0 1127.0 jit_solution(11109075200556743647)
XLA Ops:
  16.7 13.5 %all-gather = bf16[8,1,128]{2,1,0:T(2,128)(2,1)S(1)} all-gather(bf16[1,1,128]{2,1,0:T(2,128)(2,1)S(1)} %convert_bitcast_fusion.3), channel_id=1, replica_groups=mesh['seq'=4,'fsdp'=8] {'fsdp'}, dimensions={0}, use_global_device_ids=true | all-gather | bytes 2304 | tf_op jit(solution)/shard_map/all_gather | solution.py:62
  31.2 46.5 %all-gather.7.cloned.1.call-done = bf16[1024,3072]{1,0:T(8,128)(2,1)} async-done(((bf16[128,3072]{1,0:T(8,128)(2,1)}), bf16[1024,3072]{1,0:T(8,128)(2,1)}) %all-gather.7.cloned.1.call-update) | async-done | bytes 6291472 | tf_op jit(solution)/shard_map/all_gather | solution.py:63
  120.8 16.1 %collective-permute-done.1 = bf16[512,3,1,256]{3,0,1,2:T(8,128)(2,1)S(1)} collective-permute-done((bf16[512,3,1,256]{3,0,1,2:T(8,128)(2,1)}, bf16[512,3,1,256]{3,0,1,2:T(8,128)(2,1)S(1)}, u32[]{:S(2)}, u32[]{:S(2)}) %collective-permute-start.1) | collective-permute-done | bytes 786464 | tf_op jit(solution)/shard_map/ppermute | solution.py:75
  147.4 13.1 %reshape.405 = bf16[2048,3,4,64]{3,2,1,0:T(4,128)(2,1)} reshape(bf16[4,512,3,256]{3,2,1,0:T(4,128)(2,1)} %copy.173) | data formatting | bytes 6291456 | tf_op jit(solution)/shard_map/reshape;reshape | solution.py:78
  160.5 23.1 %gather_fusion.1 = bf16[2048,3,4,64]{3,2,1,0:T(4,128)(2,1)} fusion(bf16[2048,3,4,64]{3,2,1,0:T(4,128)(2,1)} %reshape.405, s32[2048]{0:T(1024)S(1)} %fusion.84), kind=kCustom, calls=%fused_computation.1 | custom fusion | bytes 6299648 | tf_op jit(solution)/shard_map/gather | solution.py:82
  198.9 64.4 %while.28 = (s32[]{:T(128)}, bf16[4,512,4,64]{1,3,2,0:T(8,128)(2,1)}, f32[4,4,512]{2,1,0:T(4,128)}, s32[4,512]{1,0:T(4,128)}, s32[2048]{0:T(1024)S(1)}, /*index=...) while((s32[]{:T(128)}, ...), condition=%wide.region_6.7_spmd.clone, body=%wide.region_3.6_spmd.clone.sunk | while | flops 1127348224 | bytes 57233532 | solution.py:116
  290.3 9.1 all-gather.1
  318.0 18.7 %fusion.90 = f32[512,8192]{1,0:T(8,128)} fusion(bf16[1024,8192]{1,0:T(8,128)(2,1)} %all-gather.11.cloned.1.call-done, f32[512,1024]{1,0:T(8,128)} %get-tuple-element.426, f32[1024]{0:T(1024)S(1)} %bitcast.256, f32[512]{0:T(512)S(1)} %get-tuple-element.424), kind=kOutput, calls=%fused_computation.152 | convolution fusion | flops 8591507456 | bytes 35657728 | tf_op jit(solution)/shard_map/dot_general | solution.py:129
  341.8 15.1 %multiply_convert_fusion.2 = (bf16[512,4096]{1,0:T(8,128)(2,1)}, bf16[512,4096]{1,0:T(8,128)(2,1)}, bf16[512,4096]{1,0:T(8,128)(2,1)S(1)}) fusion(f32[512,8192]{1,0:T(8,128)} %fusion.90, bf16[1024,4096]{1,0:T(8,128)(2,1)} %all-gather.13.cloned.1.call-done, bf16[1,512,1024]{2,1,0:T(8,128)(2,1)S(1)} %copy-done.24), kind=kOutput, calls=%fused_computation.68 | convolution fusion | flops 4326424576 | bytes 38797312 | tf_op jit(solution)/shard_map/dot_general | solution.py:148
  365.7 11.7 %copy.183 = bf16[1024,4096]{1,0:T(8,128)(2,1)} copy(bf16[1024,4096]{0,1:T(8,128)(2,1)} %convert_bitcast_fusion) | data formatting | bytes 16777216
  377.4 18.3 %multiply_reduce_fusion.1 = (bf16[1024]{0:T(1024)(128)(2,1)}, f32[512]{0:T(512)S(1)}, f32[512,1024]{1,0:T(8,128)}) fusion(f32[512,1024]{1,0:T(8,128)} %get-tuple-element.426, f32[512]{0:T(512)S(1)} %get-tuple-element.424, f32[1024]{0:T(1024)S(1)} %bitcast.257, bf16[1024,8192]{1,0:T(8,128)(2,1)} %all-gather.11.cloned.1.call-done, ...), kind=kOutput, calls=%fused_computation.99 | convolution fusion | flops 8609855488 | bytes 29370368 | tf_op jit(solution)/shard_map/rf,df->rd/dot_general | solution.py:155
  410.9 9.6 all-to-all-done.1
  424.8 16.0 %gather_fusion.3 = bf16[2048,4,64]{2,1,0:T(4,128)(2,1)} fusion(bf16[2048,4,64]{2,1,0:T(4,128)(2,1)} %reshape.407, s32[2048]{0:T(1024)S(1)} %copy-done.29), kind=kCustom, calls=%fused_computation.3 | custom fusion | bytes 2105344 | tf_op jit(solution)/shard_map/gather | solution.py:175
  445.9 208.8 %while.29 = (s32[]{:T(128)}, f32[2048,4,64]{0,2,1:T(8,128)}, f32[2048,4,64]{0,2,1:T(8,128)}, bf16[4,512,4,64]{1,3,2,0:T(8,128)(2,1)}, bf16[4,512,4,64]{1,3,2,0:T...) while((s32[]{:T(128)}, f32[2048,4,64]{0,2,1:T(8,128)}, ...), condition=%wide.region_11.12_spmd.clone, body=%wide.region_9.11_spmd.clone.sunk | while | flops 2753296384 | bytes 268841472 | solution.py:209
  453.9 12.3 %multiply_reduce_fusion.5 = (f32[4,512]{1,0:T(4,128)}, f32[4,512,2048]{2,1,0:T(8,128)}) fusion(f32[4,512,2048]{2,1,0:T(8,128)S(1)} %fusion.147, f32[4,512]{1,0:T(4,128)S(1)} %dynamic-slice_bitcast_fusion.2, pred[512,2048]{1,0:T(8,128)(4,1)S(1)} %fusion.148, bf16[2048,4,64]{0,2,1:T(8,128)(2,1)} %get-tuple-element.642, ...), kind=kOutput, calls=%fused_computation.29.clone.1 | convolution fusion | flops 557840384 | bytes 35930116 | tf_op jit(solution)/shard_map/while/body/eval_jaxpr/qhd,khd->hqk/dot_general | solution.py:188
  466.2 10.9 multiply_convert_fusion.8
  505.8 12.3 %multiply_reduce_fusion.5 = (f32[4,512]{1,0:T(4,128)}, f32[4,512,2048]{2,1,0:T(8,128)}) fusion(f32[4,512,2048]{2,1,0:T(8,128)S(1)} %fusion.147, f32[4,512]{1,0:T(4,128)S(1)} %dynamic-slice_bitcast_fusion.2, pred[512,2048]{1,0:T(8,128)(4,1)S(1)} %fusion.148, bf16[2048,4,64]{0,2,1:T(8,128)(2,1)} %get-tuple-element.642, ...), kind=kOutput, calls=%fused_computation.29.clone.1 | convolution fusion | flops 557840384 | bytes 35930116 | tf_op jit(solution)/shard_map/while/body/eval_jaxpr/qhd,khd->hqk/dot_general | solution.py:188
  518.1 10.9 multiply_convert_fusion.8
  558.0 12.3 %multiply_reduce_fusion.5 = (f32[4,512]{1,0:T(4,128)}, f32[4,512,2048]{2,1,0:T(8,128)}) fusion(f32[4,512,2048]{2,1,0:T(8,128)S(1)} %fusion.147, f32[4,512]{1,0:T(4,128)S(1)} %dynamic-slice_bitcast_fusion.2, pred[512,2048]{1,0:T(8,128)(4,1)S(1)} %fusion.148, bf16[2048,4,64]{0,2,1:T(8,128)(2,1)} %get-tuple-element.642, ...), kind=kOutput, calls=%fused_computation.29.clone.1 | convolution fusion | flops 557840384 | bytes 35930116 | tf_op jit(solution)/shard_map/while/body/eval_jaxpr/qhd,khd->hqk/dot_general | solution.py:188
  570.3 10.9 multiply_convert_fusion.8
  610.2 12.3 %multiply_reduce_fusion.5 = (f32[4,512]{1,0:T(4,128)}, f32[4,512,2048]{2,1,0:T(8,128)}) fusion(f32[4,512,2048]{2,1,0:T(8,128)S(1)} %fusion.147, f32[4,512]{1,0:T(4,128)S(1)} %dynamic-slice_bitcast_fusion.2, pred[512,2048]{1,0:T(8,128)(4,1)S(1)} %fusion.148, bf16[2048,4,64]{0,2,1:T(8,128)(2,1)} %get-tuple-element.642, ...), kind=kOutput, calls=%fused_computation.29.clone.1 | convolution fusion | flops 557840384 | bytes 35930116 | tf_op jit(solution)/shard_map/while/body/eval_jaxpr/qhd,khd->hqk/dot_general | solution.py:188
  622.5 10.9 multiply_convert_fusion.8
  676.8 9.5 pad_maximum_fusion.3
  686.3 18.7 %gather_fusion.4 = bf16[2048,3,256]{2,1,0:T(4,128)(2,1)} fusion(bf16[2048,3,256]{2,1,0:T(4,128)(2,1)} %pad_maximum_fusion.3, s32[2048]{0:T(1024)S(1)} %copy-done.27), kind=kCustom, calls=%fused_computation.4 | custom fusion | bytes 6299648 | tf_op jit(solution)/shard_map/gather | solution.py:222
  705.0 51.6 %all_to_all.45 = bf16[2048,3,1,256]{3,1,2,0:T(4,128)(2,1)S(1)} all-to-all(bf16[2048,3,1,256]{3,1,2,0:T(4,128)(2,1)} %bitcast.233), channel_id=1, replica_groups=mesh['seq'=4,'fsdp'=8] {'seq'}, dimensions={0} | all-to-all | bytes 6291456 | tf_op jit(solution)/shard_map/all_to_all | solution.py:223
  770.0 16.7 %convolution_convert_fusion = bf16[1024,8192]{1,0:T(8,128)(2,1)} fusion(bf16[512,4096]{1,0:T(8,128)(2,1)} %get-tuple-element.412, bf16[512,4096]{1,0:T(8,128)(2,1)} %get-tuple-element.411, f32[512,1024]{1,0:T(8,128)S(1)} %copy-done.12, f32[1024]{0:T(1024)S(1)} %bitcast.259, f32[512]{0:T(512)S(1)} %copy-done.38), kind=kOutput, calls=%fused_computation.64 | convolution fusion | flops 8616673280 | bytes 27269120 | tf_op jit(solution)/shard_map/rd,rf->df/dot_general | solution.py:152
  789.3 45.8 %reduce-scatter.7.cloned.1.call-done = bf16[128,3072]{1,0:T(8,128)(2,1)} async-done(((bf16[1024,3072]{1,0:T(8,128)(2,1)}), bf16[128,3072]{1,0:T(8,128)(2,1)}) %reduce-scatter.7.cloned.1.call-update) | async-done | bytes 786448 | tf_op jit(solution)/shard_map/reduce_scatter | solution.py:236
  835.1 169.0 %reduce-scatter.11.cloned.1.call-done = bf16[128,8192]{1,0:T(8,128)(2,1)} async-done(((bf16[1024,8192]{1,0:T(8,128)(2,1)}), bf16[128,8192]{1,0:T(8,128)(2,1)}) %reduce-scatter.11.cloned.1.call-update) | async-done | bytes 2097168 | tf_op jit(solution)/shard_map/reduce_scatter | solution.py:247
  1005.3 10.3 fusion.69
  1023.6 13.6 %all-reduce.2 = (bf16[1024]{0:T(1024)(128)(2,1)S(1)}, bf16[1024]{0:T(1024)(128)(2,1)S(1)}) all-reduce(bf16[1024]{0:T(1024)(128)(2,1)S(1)} %get-tuple-element.351, bf16[1024]{0:T(1024)(128)(2,1)S(1)} %copy-done.40), channel_id=2, replica_groups=mesh['seq'=4,'fsdp'=8] {'fsdp'}, use_global_device_ids=true, to_apply=%region_14.15.clone | all-reduce | flops 2048 | bytes 8192
  1037.4 10.2 all-reduce.3
  1051.7 59.8 %all-reduce.7.cloned.1.call-done = (bf16[128,4096]{0,1:T(8,128)(2,1)}, bf16[128,3072]{1,0:T(8,128)(2,1)}, bf16[128,1024]{1,0:T(8,128)(2,1)}, bf16[128,8192]{1,0:T(8,128)(2,1)}) async-done(((bf16[128,4096]{0,1:T(8,128)(2,1)}, bf16[128,3072]{1,0:T(8,128)(2,1)}, bf16[128,1024]{1,0:T(8,128)(2,1)}, bf16[128,8192]{1,0:T(8,128)(2,1)}), (bf16[128,4096]{0,1:T(8,128)(2,1)}, bf16[128,3072]{1,0:T(8,128)(2,1)}, ...) | async-done | bytes 4194320 | tf_op jit(solution)/shard_map/psum | solution.py:260
  (333 shorter events, 401.4 us)
Async XLA Ops:
  7.2 70.6 %all-gather.7.cloned.1.call-start = ((), (), s32[]{:S(2)}) async-start(), calls=%async_computation.7 | async-start | bytes 7077888 | tf_op jit(solution)/shard_map/all_gather | solution.py:63
  9.6 303.8 %all-gather.9.cloned.1.call-start = ((), (), s32[]{:S(2)}) async-start(), calls=%async_computation.8 | async-start | bytes 2359296 | tf_op jit(solution)/shard_map/all_gather | solution.py:64
  11.5 306.5 %all-gather.11.cloned.1.call-start = ((), (), s32[]{:S(2)}) async-start(), calls=%async_computation.9 | async-start | bytes 18874368 | tf_op jit(solution)/shard_map/all_gather | solution.py:124
  15.4 15.7 %copy-start.41 = (s32[1,3]{1,0:T(1,128)S(1)}, s32[1,3]{1,0:T(1,128)}, u32[]{:S(2)}) copy-start(s32[1,3]{1,0:T(1,128)} %param.25) | copy-start | bytes 40
  15.4 15.7 %copy-start.43 = (s32[1,3]{1,0:T(1,128)S(1)}, s32[1,3]{1,0:T(1,128)}, u32[]{:S(2)}) copy-start(s32[1,3]{1,0:T(1,128)} %param.24) | copy-start | bytes 40
  15.5 326.3 %all-gather.13.cloned.1.call-start = ((), (), s32[]{:S(2)}) async-start(), calls=%async_computation.10 | async-start | bytes 9437184 | tf_op jit(solution)/shard_map/all_gather | solution.py:125
  30.2 47.5 %copy-start.32 = (f32[8,1,128]{2,1,0:T(1,128)}, f32[8,1,128]{2,1,0:T(1,128)S(1)}, u32[]{:S(2)}) copy-start(f32[8,1,128]{2,1,0:T(1,128)S(1)} %convert_element_type.214) | copy-start | bytes 12292
  31.1 46.6 %copy-start.35 = (f32[512]{0:T(512)}, f32[512]{0:T(512)S(1)}, u32[]{:S(2)}) copy-start(f32[512]{0:T(512)S(1)} %get-tuple-element.422) | copy-start | bytes 6148
  98.3 16.7 %copy-start.14 = (bf16[512,3,1,1,256]{4,2,1,0,3:T(2,128)(2,1)S(1)}, bf16[512,3,1,1,256]{4,2,1,0,3:T(2,128)(2,1)}, u32[]{:S(2)}) copy-start(bf16[512,3,1,1,256]{4,2,1,0,3:T(2,128)(2,1)} %get-tuple-element.417) | copy-start | bytes 2359300
  99.3 21.5 %collective-permute-start.2 = (bf16[512,3,1,256]{3,0,1,2:T(8,128)(2,1)}, bf16[512,3,1,256]{3,0,1,2:T(8,128)(2,1)S(1)}, u32[]{:S(2)}, u32[]{:S(2)}) collective-permute-start(bf16[512,3,1,256]{3,0,1,2:T(8,128)(2,1)} %bitcast.183), channel_id=1, source_target_pairs={{0,24},{8,16},{16,8},{24,0},{1,25},{9,17},{17,9},{25,1},{2,26},{10... | collective-permute-start | bytes 2359304 | tf_op jit(solution)/shard_map/ppermute | solution.py:75
  102.7 34.3 %collective-permute-start.1 = (bf16[512,3,1,256]{3,0,1,2:T(8,128)(2,1)}, bf16[512,3,1,256]{3,0,1,2:T(8,128)(2,1)S(1)}, u32[]{:S(2)}, u32[]{:S(2)}) collective-permute-start(bf16[512,3,1,256]{3,0,1,2:T(8,128)(2,1)} %bitcast.184), channel_id=1, source_target_pairs={{0,16},{8,24},{16,0},{24,8},{1,17},{9,25},{17,1},{25,9},{2,18},{10... | collective-permute-start | bytes 2359304 | tf_op jit(solution)/shard_map/ppermute | solution.py:75
  104.3 32.8 %collective-permute-start = (bf16[512,3,1,256]{3,0,1,2:T(8,128)(2,1)}, bf16[512,3,1,256]{3,0,1,2:T(8,128)(2,1)}, u32[]{:S(2)}, u32[]{:S(2)}) collective-permute-start(bf16[512,3,1,256]{3,0,1,2:T(8,128)(2,1)} %bitcast.185), channel_id=1, source_target_pairs={{0,8},{8,0},{16,24},{24,16},{1,9},{9,1},{17,25},{25,17},{2,10},{10... | collective-permute-start | bytes 2359304 | tf_op jit(solution)/shard_map/ppermute | solution.py:75
  115.0 45.5 %copy-start.28 = (s32[2048]{0:T(1024)}, s32[2048]{0:T(1024)S(1)}, u32[]{:S(2)}) copy-start(s32[2048]{0:T(1024)S(1)} %fusion.84) | copy-start | bytes 24580
  286.0 18.1 %all-to-all-start = ((bf16[4,2,65536]{2,1,0:T(2,128)(2,1)}), bf16[4,2,65536]{2,1,0:T(2,128)(2,1)}, u32[]{:S(2)}, u32[]{:S(2)}) async-start(bf16[4,2,65536]{2,1,0:T(2,128)(2,1)} %reshape.418), calls=%async_computation | async-start | bytes 2097152 | tf_op jit(solution)/shard_map/all_to_all | solution.py:118
  290.3 496.5 %reduce-scatter.13.cloned.1.call-start = ((), (), s32[]{:S(2)}) async-start(), calls=%async_computation.14 | async-start | bytes 9437184
  299.5 96.2 %copy-start.30 = (f32[8,1,128]{2,1,0:T(1,128)}, f32[8,1,128]{2,1,0:T(1,128)S(1)}, u32[]{:S(2)}) copy-start(f32[8,1,128]{2,1,0:T(1,128)S(1)} %convert_element_type.215) | copy-start | bytes 12292
  318.0 77.7 %copy-start.37 = (f32[512]{0:T(512)}, f32[512]{0:T(512)S(1)}, u32[]{:S(2)}) copy-start(f32[512]{0:T(512)S(1)} %get-tuple-element.424) | copy-start | bytes 6148
  318.0 23.7 %copy-start.24 = (bf16[1,512,1024]{2,1,0:T(8,128)(2,1)S(1)}, bf16[1,512,1024]{2,1,0:T(8,128)(2,1)}, u32[]{:S(2)}) copy-start(bf16[1,512,1024]{2,1,0:T(8,128)(2,1)} %param.22) | copy-start | bytes 3145732
  402.6 17.9 %all-to-all-start.1 = ((bf16[512,4,256]{0,2,1:T(8,128)(2,1)}), bf16[512,4,256]{0,2,1:T(8,128)(2,1)S(1)}, u32[]{:S(2)}, u32[]{:S(2)}) async-start(bf16[512,4,256]{0,2,1:T(8,128)(2,1)} %bitcast.241), calls=%async_computation.1 | async-start | bytes 2097152 | tf_op jit(solution)/shard_map/all_to_all | solution.py:172
  406.3 383.0 %reduce-scatter.9.cloned.1.call-start = ((), (), s32[]{:S(2)}) async-start(), calls=%async_computation.12 | async-start | bytes 2359296 | tf_op jit(solution)/shard_map/reduce_scatter | solution.py:239
  410.8 424.2 %reduce-scatter.7.cloned.1.call-start = ((), (), s32[]{:S(2)}) async-start(), calls=%async_computation.11 | async-start | bytes 7077888 | tf_op jit(solution)/shard_map/reduce_scatter | solution.py:236
  450.4 15.8 %copy-start = (f32[4,512,2048]{2,1,0:T(8,128)}, f32[4,512,2048]{2,1,0:T(8,128)S(1)}, u32[]{:S(2)}) copy-start(f32[4,512,2048]{2,1,0:T(8,128)S(1)} %fusion.147) | copy-start | bytes 50331652 | tf_op jit(solution)/shard_map/while
  502.3 15.8 %copy-start = (f32[4,512,2048]{2,1,0:T(8,128)}, f32[4,512,2048]{2,1,0:T(8,128)S(1)}, u32[]{:S(2)}) copy-start(f32[4,512,2048]{2,1,0:T(8,128)S(1)} %fusion.147) | copy-start | bytes 50331652 | tf_op jit(solution)/shard_map/while
  529.0 15.7 %slice-start = ((s8[8388608]{0:T(1024)(128)(4,1)}), s8[4194304]{0:T(1024)(128)(4,1)S(1)}, s32[]{:S(2)}) async-start(s8[8388608]{0:T(1024)(128)(4,1)} %bitcast.231), calls=%async_computation.16 | async-start | bytes 8388608 | tf_op jit(solution)/shard_map/while
  554.5 15.8 %copy-start = (f32[4,512,2048]{2,1,0:T(8,128)}, f32[4,512,2048]{2,1,0:T(8,128)S(1)}, u32[]{:S(2)}) copy-start(f32[4,512,2048]{2,1,0:T(8,128)S(1)} %fusion.147) | copy-start | bytes 50331652 | tf_op jit(solution)/shard_map/while
  581.2 15.7 %slice-start = ((s8[8388608]{0:T(1024)(128)(4,1)}), s8[4194304]{0:T(1024)(128)(4,1)S(1)}, s32[]{:S(2)}) async-start(s8[8388608]{0:T(1024)(128)(4,1)} %bitcast.231), calls=%async_computation.16 | async-start | bytes 8388608 | tf_op jit(solution)/shard_map/while
  606.7 15.8 %copy-start = (f32[4,512,2048]{2,1,0:T(8,128)}, f32[4,512,2048]{2,1,0:T(8,128)S(1)}, u32[]{:S(2)}) copy-start(f32[4,512,2048]{2,1,0:T(8,128)S(1)} %fusion.147) | copy-start | bytes 50331652 | tf_op jit(solution)/shard_map/while
  768.4 235.6 %reduce-scatter.11.cloned.1.call-start = ((), (), s32[]{:S(2)}) async-start(), calls=%async_computation.13 | async-start | bytes 18874368 | tf_op jit(solution)/shard_map/reduce_scatter | solution.py:247
  786.7 217.4 %copy-start.45 = (u32[32]{0:T(128)S(1)}, u32[32]{0:T(128)}, u32[]{:S(2)}) copy-start(u32[32]{0:T(128)} %constant.88) | copy-start | bytes 388
  786.7 324.9 %all-reduce.7.cloned.1.call-start = ((), (), s32[]{:S(2)}) async-start(), calls=%async_computation.15 | async-start | bytes 8388608 | tf_op jit(solution)/shard_map/psum | solution.py:260
  1015.6 33.0 %copy-start.11 = (f32[512,1024]{1,0:T(8,128)S(1)}, f32[512,1024]{1,0:T(8,128)}, u32[]{:S(2)}) copy-start(f32[512,1024]{1,0:T(8,128)} %copy-done.10) | copy-start | bytes 6291460
  1015.7 33.0 %copy-start.34 = (f32[512]{0:T(512)S(1)}, f32[512]{0:T(512)}, u32[]{:S(2)}) copy-start(f32[512]{0:T(512)} %get-tuple-element.421) | copy-start | bytes 6148
  (64 other events, 387.4 us)
Sparse Core Ops, SparseCore 0:
  10.2 67.4 all-gather.6
  79.9 27.7 all-gather.8
  109.3 150.5 all-gather.10
  261.4 80.3 all-gather.12
  377.5 88.0 reduce-scatter.12
  467.8 34.1 reduce-scatter.8
  768.5 66.4 reduce-scatter.6
  837.4 166.5 reduce-scatter.10
  1008.3 103.2 all-reduce.6
